TPU v7x, 128 devices: a whole 4x4x4 slice. The times are simulated.
128 devices in a mesh: dp: 4 (over x), clus: 32 (over y, z, core).
Axes of the slice: x: 4, y: 4, z: 4, core: 2. Of those that a mesh axis runs over, the one named last changes fastest.
Arguments:
- embeddings: bfloat16 [65536, 1024], P(('dp', 'clus')), may hold values from -8 to 8
- parents: int32 [65536, 8], P(('dp', 'clus')), may hold values from 0 to 255, all different within a row; in each aligned block of 512 rows (0 to 511, 512 to 1023, ...) at most 32 rows name the same one
- children: int32 [65536, 8], P(('dp', 'clus')), may hold values from 0 to 1
- temper: float32 [256], P('clus'), may hold values from 0.5 to 2
- level_two: bfloat16 [32768, 1024], P('clus'), may hold values from -2 to 2
- level_three: bfloat16 [65536, 1024], P('clus'), may hold values from -0.1875 to 0.1875
Outputs:
- soft_codes: bfloat16 [65536, 1024], P(('dp', 'clus'))
- candidate_scores: float32 [65536, 1024], P(('dp', 'clus'))
- new_centroids: float32 [32768, 1024], P('clus')
- cluster_mass: float32 [32768], P('clus')
Inputs may be any that keep to these rules, and one draw needn't show every extreme that they name: `parents`: each row names 8 different blocks. Among the rows of one device no block is named by more than 32 rows, and in every draw some block is named by exactly 32 rows of one device.
All inputs are finite; a program needn't handle non-finite values.
Results may differ from a plain program's by a relative error of at most 0.0045.
Values may be sent and summed in bfloat16 or wider, within the bound.
A program may use at most 192 MiB of HBM per device.

v0:
```python
import math
import jax
import jax.numpy as jnp
from jax import lax
from jax.sharding import PartitionSpec as P


def local_ranks(block_ids, first_block, block_count):
    length = block_ids.shape[-1]
    group = math.gcd(length, 128)
    groups = length // group
    leading = block_ids.shape[:-1]
    onehot = (
        (block_ids - first_block)[..., None] == jnp.arange(block_count, dtype=jnp.int32)
    ).astype(jnp.bfloat16)
    grouped = onehot.reshape(leading + (groups, group, block_count))
    lower = (jnp.arange(group)[:, None] > jnp.arange(group)[None, :]).astype(jnp.bfloat16)
    within = jnp.einsum("ij,...gjb->...gib", lower, grouped, preferred_element_type=jnp.float32)
    group_sums = jnp.sum(grouped, axis=-2, dtype=jnp.float32)
    earlier = (jnp.arange(groups)[:, None] > jnp.arange(groups)[None, :]).astype(jnp.float32)
    before = jnp.einsum("hg,...gb->...hb", earlier, group_sums, precision=lax.Precision.HIGHEST)
    counted = within + before[..., None, :]
    position = jnp.sum(counted * grouped.astype(jnp.float32), axis=-1).reshape(leading + (length,))
    return (onehot, position)


def slot_table(onehot, position, most_rows):
    length = position.shape[-1]
    rank_hot = (position[..., None] == jnp.arange(most_rows, dtype=jnp.float32)).astype(jnp.float32)
    numbers = jnp.arange(length, dtype=jnp.float32) + 1.0
    located = jnp.einsum(
        "...nb,...nk->...bk",
        onehot.astype(jnp.float32),
        rank_hot * numbers[:, None],
        precision=lax.Precision.HIGHEST,
    )
    located = located.reshape(located.shape[:-2] + (located.shape[-2] * located.shape[-1],))
    return (located + 0.5).astype(jnp.int32) - 1


def body(embeddings, parents, children, temper, level_two, level_three):
    row_count, features = embeddings.shape
    parent_count = parents.shape[1]
    blocks_here = temper.shape[0]
    block_size = level_two.shape[0] // blocks_here
    child_count = level_three.shape[0] // (blocks_here * block_size)
    shard_count = lax.axis_size("clus")
    own_index = lax.axis_index("clus")
    all_blocks = blocks_here * shard_count
    most_rows = 2 * row_count * parent_count // all_blocks
    item_count = row_count * parent_count
    slot_count = blocks_here * most_rows
    flat_blocks = parents.reshape(item_count)
    own_onehot, own_position = local_ranks(flat_blocks, 0, all_blocks)
    global_slot = flat_blocks * most_rows + own_position.astype(jnp.int32)
    own_item = slot_table(own_onehot, own_position, most_rows)
    own_filled = own_item >= 0
    own_safe = jnp.maximum(own_item, 0)
    all_rows, all_parents, all_children = (
        lax.all_gather(embeddings, "clus", axis=0, tiled=True),
        lax.all_gather(parents, "clus", axis=0, tiled=True),
        lax.all_gather(children, "clus", axis=0, tiled=True),
    )
    source_blocks = all_parents.reshape(shard_count, item_count)
    mine_onehot, mine_position = local_ranks(source_blocks, own_index * blocks_here, blocks_here)
    local_table = slot_table(mine_onehot, mine_position, most_rows)
    sources = jnp.arange(shard_count, dtype=jnp.int32)[:, None]
    slot_item = jnp.where(local_table >= 0, sources * item_count + local_table, -1).reshape(-1)
    filled = slot_item >= 0
    safe_item = jnp.maximum(slot_item, 0)
    slot_rows = jnp.where(filled[:, None], jnp.take(all_rows, safe_item // parent_count, axis=0), 0)
    slot_child = jnp.where(filled, all_children.reshape(-1)[safe_item], -1)
    slot_rows = slot_rows.reshape(shard_count, blocks_here, most_rows, features)
    slot_child = slot_child.reshape(shard_count, blocks_here, most_rows)
    centroids = level_two.reshape(blocks_here, block_size, features)
    scores = jnp.einsum("sbmd,bcd->sbmc", slot_rows, centroids, preferred_element_type=jnp.float32)
    scores = scores * temper[None, :, None, None]
    third = level_three.reshape(blocks_here, child_count, block_size, features)
    deeper = jnp.zeros(scores.shape, jnp.float32)
    for child in range(child_count):
        product = jnp.einsum(
            "sbmd,bcd->sbmc", slot_rows, third[:, child], preferred_element_type=jnp.float32
        )
        deeper = jnp.where((slot_child == child)[..., None], product, deeper)
    back_scores, back_deeper = (
        lax.all_to_all(scores, "clus", split_axis=0, concat_axis=0, tiled=True),
        lax.all_to_all(deeper, "clus", split_axis=0, concat_axis=0, tiled=True),
    )
    item_scores = back_scores.reshape(all_blocks * most_rows, block_size)[global_slot].reshape(
        row_count, parent_count * block_size
    )
    item_deeper = back_deeper.reshape(all_blocks * most_rows, block_size)[global_slot].reshape(
        row_count, parent_count, block_size
    )
    top = jnp.max(item_scores, axis=1, keepdims=True)
    weights = jnp.exp(item_scores - top)
    total = jnp.sum(weights, axis=1, keepdims=True)
    probs = weights / total
    soft_codes = probs.astype(jnp.bfloat16)
    mass = probs.reshape(row_count, parent_count, block_size).sum(axis=2)
    candidate_scores = (parent_count * mass[:, :, None] * item_deeper).reshape(
        row_count, parent_count * block_size
    )
    code_items = probs.reshape(item_count, block_size)
    send_codes = jnp.where(own_filled[:, None], code_items[own_safe], 0.0)
    owner_codes = lax.all_to_all(
        send_codes.reshape(shard_count, slot_count, block_size),
        "clus",
        split_axis=0,
        concat_axis=0,
        tiled=True,
    )
    owner_codes = owner_codes.reshape(shard_count, blocks_here, most_rows, block_size)
    code_high = owner_codes.astype(jnp.bfloat16)
    code_low = (owner_codes - code_high.astype(jnp.float32)).astype(jnp.bfloat16)
    code_pair = jnp.concatenate([code_high, code_low], axis=-1)
    pair_sums = jnp.einsum(
        "sbmc,sbmd->bcd", code_pair, slot_rows, preferred_element_type=jnp.float32
    )
    partial_sums = pair_sums[:, :block_size] + pair_sums[:, block_size:]
    partial_mass = jnp.sum(owner_codes, axis=(0, 2))
    weighted, cluster_mass = lax.psum((partial_sums, partial_mass), "dp")
    cluster_mass = cluster_mass.reshape(blocks_here * block_size)
    new_centroids = (
        weighted.reshape(blocks_here * block_size, features)
        / jnp.maximum(cluster_mass, 1.0)[:, None]
    )
    return (soft_codes, candidate_scores, new_centroids, cluster_mass)


def solution(mesh):
    in_specs = (
        P(("dp", "clus"), None),
        P(("dp", "clus"), None),
        P(("dp", "clus"), None),
        P("clus"),
        P("clus", None),
        P("clus", None),
    )
    out_specs = (P(("dp", "clus"), None), P(("dp", "clus"), None), P("clus", None), P("clus"))
    return jax.shard_map(body, mesh=mesh, in_specs=in_specs, out_specs=out_specs, check_vma=False)
```

profile of v0, /device:TPU:1, one launch (start us, length us, event | category | flops | bytes accessed | tf_op | source)
XLA Modules:
  0.0 820.3 jit_solution(16947258658350363316)
XLA Ops:
  7.9 28.2 %all_gather.9 = s32[16384,8]{0,1:T(8,128)S(1)} all-gather(s32[512,8]{0,1:T(8,128)} %param.7), channel_id=1, replica_groups=mesh['dp'=4,'clus'=32] {'clus'}, dimensions={0}, use_global_device_ids=true | all-gather | bytes 540672 | tf_op jit(solution)/shard_map/all_gather | solution.py:61
  41.3 6.4 sub.61
  47.7 7.6 sub.60
  60.5 9.0 %fusion.34 = s32[32,8,32]{2,1,0:T(8,128)S(1)} fusion(f32[4096]{0:T(1024)S(1)} %iota_add_fusion, f32[32,4096]{1,0:T(8,128)S(1)} %bitcast.88, s32[32,4096]{1,0:T(8,128)S(1)} %copy-done.5), kind=kOutput, calls=%fused_computation.55 | convolution fusion | flops 412114944 | bytes 1097728 | tf_op jit(solution)/shard_map/...nb,...nk->...bk/dot_general | solution.py:31
  69.6 25.6 %all_gather.11 = s32[16384,8]{0,1:T(8,128)S(1)} all-gather(s32[512,8]{0,1:T(8,128)S(1)} %copy-done.7), channel_id=1, replica_groups=mesh['dp'=4,'clus'=32] {'clus'}, dimensions={0}, use_global_device_ids=true | all-gather | bytes 540672 | tf_op jit(solution)/shard_map/all_gather | solution.py:62
  95.2 5.4 copy.73
  100.6 6.7 reshape.338
  107.5 45.5 %gather_fusion.2 = s32[8192]{0:T(1024)S(1)} fusion(s32[131072]{0:T(1024)S(1)} %reshape.338, s32[8192]{0:T(1024)S(1)} %broadcast_clamp_fusion.1), kind=kCustom, calls=%fused_computation.2 | custom fusion | bytes 98304 | tf_op jit(solution)/shard_map/gather | solution.py:72
  153.7 240.2 %gather_fusion = bf16[8192,1024]{1,0:T(8,128)(2,1)} fusion(bf16[16384,1024]{1,0:T(8,128)(2,1)} %all-gather.2.cloned.1.call-done, s32[8192]{0:T(1024)S(1)} %broadcast_clamp_fusion.2), kind=kCustom, calls=%fused_computation | custom fusion | bytes 33587200 | tf_op jit(solution)/shard_map/jit(_take)/gather | solution.py:71
  393.9 21.6 %multiply_bitcast_fusion = f32[32,8,32,128]{3,0,2,1:T(8,128)S(1)} fusion(f32[8]{0:T(128)S(1)} %copy-done.10, bf16[8,128,1024,1]{2,1,3,0:T(8,128)(2,1)S(1)} %bitcast.79, bf16[32,8,32,1024]{3,2,1,0:T(8,128)(2,1)} %bitcast.80, pred[32,8,32]{0,2,1:T(8,128)(4,1)S(1)} %copy.68, pred[32,8,32]{0,2,1:T(8,128)(4,1)S(1)} %copy.67), kind=kOutput, calls=%fused_computation.31 | convolution fusion | flops 2165309440 | bytes 23085088 | tf_op jit(solution)/shard_map/sbmd,bcd->sbmc/dot_general | solution.py:76
  420.0 89.5 %all-to-all-start = ((f32[32,8,32,128]{3,2,1,0:T(8,128)}), f32[32,8,32,128]{3,2,1,0:T(8,128)}, u32[]{:S(2)}, u32[]{:S(2)}) async-start(f32[32,8,32,128]{3,2,1,0:T(8,128)} %copy.70), calls=%async_computation | async-start | bytes 8388608 | tf_op jit(solution)/shard_map/all_to_all | solution.py:86
  515.2 46.3 %all-to-all-done = f32[32,8,32,128]{3,2,1,0:T(8,128)} async-done(((f32[32,8,32,128]{3,2,1,0:T(8,128)}), f32[32,8,32,128]{3,2,1,0:T(8,128)}, u32[]{:S(2)}, u32[]{:S(2)}) %all-to-all-start) | async-done | bytes 4194336 | tf_op jit(solution)/shard_map/all_to_all | solution.py:86
  561.5 13.0 %gather_fusion.1 = f32[4096,128]{1,0:T(8,128)S(1)} fusion(f32[8192,128]{1,0:T(8,128)} %bitcast.11, s32[4096]{0:T(1024)S(1)} %broadcast_clamp_fusion.3), kind=kCustom, calls=%fused_computation.1 | custom fusion | bytes 4210688 | tf_op jit(solution)/shard_map/gather | solution.py:89
  580.7 28.0 %gather_fusion.4 = f32[8192,128]{1,0:T(8,128)} fusion(f32[4096,128]{1,0:T(8,128)S(1)} %get-tuple-element.7, s32[8192]{0:T(1024)S(1)} %broadcast_clamp_fusion), kind=kCustom, calls=%fused_computation.4 | custom fusion | bytes 8421376 | tf_op jit(solution)/shard_map/gather | solution.py:105
  613.9 7.5 all-to-all-start.2
  621.4 21.8 %fusion.21 = f32[8,32,32,128]{3,1,2,0:T(8,128)S(1)} fusion(bf16[8,2,128,1024]{3,2,1,0:T(8,128)(2,1)} %bitcast.97, bf16[32,8,32,1024]{3,2,1,0:T(8,128)(2,1)} %bitcast.81, pred[32,8,32]{0,2,1:T(8,128)(4,1)S(1)} %copy.68, pred[32,8,32]{0,2,1:T(8,128)(4,1)S(1)} %copy.67), kind=kOutput, calls=%fused_computation.41 | convolution fusion | flops 2164260864 | bytes 23085056 | tf_op jit(solution)/shard_map/sbmd,bcd->sbmc/dot_general | solution.py:81
  643.2 17.8 %fusion.12 = f32[32,8,32,128]{3,0,2,1:T(8,128)S(1)} fusion(f32[8,32,32,128]{3,1,2,0:T(8,128)S(1)} %fusion.21, bf16[8,2,128,1024]{3,2,1,0:T(8,128)(2,1)S(1)} %bitcast.98, pred[32,8,32]{0,2,1:T(8,128)(4,1)S(1)} %copy.76, pred[32,8,32]{0,2,1:T(8,128)(4,1)S(1)} %copy.74, bf16[32,8,32,1024]{3,2,1,0:T(8,128)(2,1)} %bitcast.82, pred[32,8,32]{0,2,1:T(8,128)(4,1)S(1)} %copy.68, ...), kind=kOutput, calls=%fused_computation.25 | convolution fusion | flops 2166358016 | bytes 27394048 | tf_op jit(solution)/shard_map/sbmd,bcd->sbmc/dot_general | solution.py:81
  665.5 7.8 all-to-all-done.2
  673.3 7.1 all-to-all-start.1
  685.8 22.2 %fusion.18 = f32[8,256,1024]{2,1,0:T(8,128)S(1)} fusion(bf16[32,8,32,128]{3,0,2,1:T(8,128)(2,1)S(1)} %get-tuple-element.4, bf16[32,8,32,128]{3,0,2,1:T(8,128)(2,1)S(1)} %get-tuple-element.5, bf16[32,8,32,1024]{3,2,1,0:T(8,128)(2,1)} %bitcast.83, pred[32,8,32]{0,2,1:T(8,128)(4,1)S(1)} %copy.68, pred[32,8,32]{0,2,1:T(8,128)(4,1)S(1)} %copy.67), kind=kOutput, calls=%fused_computation.37 | convolution fusion | flops 4320133120 | bytes 29376512 | tf_op jit(solution)/shard_map/sbmc,sbmd->bcd/dot_general | solution.py:117
  714.0 18.4 %all-to-all-done.1 = f32[32,8,32,128]{3,2,1,0:T(8,128)} async-done(((f32[32,8,32,128]{3,2,1,0:T(8,128)}), f32[32,8,32,128]{3,2,1,0:T(8,128)}, u32[]{:S(2)}, u32[]{:S(2)}) %all-to-all-start.1) | async-done | bytes 4194336 | tf_op jit(solution)/shard_map/all_to_all | solution.py:87
  732.5 16.5 %gather_fusion.3 = f32[4096,128]{1,0:T(8,128)} fusion(f32[8192,128]{1,0:T(8,128)} %bitcast.26, s32[4096]{0:T(1024)S(1)} %broadcast_clamp_fusion.3), kind=kCustom, calls=%fused_computation.3 | custom fusion | bytes 4210688 | tf_op jit(solution)/shard_map/gather | solution.py:92
  759.5 12.3 %psum.15 = f32[1024]{0:T(1024)S(1)} all-reduce(f32[1024]{0:T(1024)S(1)} %bitcast.95), channel_id=1, replica_groups=mesh['dp'=4,'clus'=32] {'dp'}, use_global_device_ids=true, to_apply=%region_12.13 | all-reduce | flops 1024 | bytes 8192 | tf_op jit(solution)/shard_map/psum | solution.py:122
  771.8 36.5 %all-reduce.2.cloned.1.call-done = f32[1024,1024]{1,0:T(8,128)} async-done(((f32[1024,1024]{1,0:T(8,128)}), f32[1024,1024]{1,0:T(8,128)}) %all-reduce.2.cloned.1.call-update) | async-done | bytes 4194320 | tf_op jit(solution)/shard_map/psum | solution.py:122
  (96 shorter events, 64.3 us)
Async XLA Ops:
  7.2 386.8 %copy-start = (bf16[1024,1024]{1,0:T(8,128)(2,1)S(1)}, bf16[1024,1024]{1,0:T(8,128)(2,1)}, u32[]{:S(2)}) copy-start(bf16[1024,1024]{1,0:T(8,128)(2,1)} %param.10) | copy-start | bytes 6291460
  7.2 146.5 %all-gather.2.cloned.1.call-start = ((), (), s32[]{:S(2)}) async-start(), calls=%async_computation.3 | async-start | bytes 34603008 | tf_op jit(solution)/shard_map/all_gather | solution.py:60
  57.2 3.2 copy-start.5
  60.4 9.2 %copy-start.7 = (s32[512,8]{0,1:T(8,128)S(1)}, s32[512,8]{0,1:T(8,128)}, u32[]{:S(2)}) copy-start(s32[512,8]{0,1:T(8,128)} %param.8) | copy-start | bytes 49156
  153.7 240.2 %copy-start.10 = (f32[8]{0:T(128)S(1)}, f32[8]{0:T(128)}, u32[]{:S(2)}) copy-start(f32[8]{0:T(128)} %param.9) | copy-start | bytes 100
  420.0 89.6 %copy-start.6 = (s32[512,8]{0,1:T(8,128)S(1)}, s32[512,8]{0,1:T(8,128)}, u32[]{:S(2)}) copy-start(s32[512,8]{0,1:T(8,128)} %param.7) | copy-start | bytes 49156
  420.0 141.5 %all-to-all-start = ((f32[32,8,32,128]{3,2,1,0:T(8,128)}), f32[32,8,32,128]{3,2,1,0:T(8,128)}, u32[]{:S(2)}, u32[]{:S(2)}) async-start(f32[32,8,32,128]{3,2,1,0:T(8,128)} %copy.70), calls=%async_computation | async-start | bytes 8388608 | tf_op jit(solution)/shard_map/all_to_all | solution.py:86
  574.5 3.0 copy-start.2
  613.9 59.4 %all-to-all-start.2 = ((f32[32,256,128]{2,1,0:T(8,128)}), f32[32,256,128]{2,1,0:T(8,128)}, u32[]{:S(2)}, u32[]{:S(2)}) async-start(f32[32,256,128]{2,1,0:T(8,128)} %broadcast_select_fusion), calls=%async_computation.2 | async-start | bytes 8388608 | tf_op jit(solution)/shard_map/all_to_all | solution.py:106
  621.4 21.8 %copy-start.9 = (bf16[2048,1024]{1,0:T(8,128)(2,1)S(1)}, bf16[2048,1024]{1,0:T(8,128)(2,1)}, u32[]{:S(2)}) copy-start(bf16[2048,1024]{1,0:T(8,128)(2,1)} %param.11) | copy-start | bytes 12582916
  673.3 59.2 %all-to-all-start.1 = ((f32[32,8,32,128]{3,2,1,0:T(8,128)}), f32[32,8,32,128]{3,2,1,0:T(8,128)}, u32[]{:S(2)}, u32[]{:S(2)}) async-start(f32[32,8,32,128]{3,2,1,0:T(8,128)} %copy.78), calls=%async_computation.1 | async-start | bytes 8388608 | tf_op jit(solution)/shard_map/all_to_all | solution.py:87
  680.4 127.9 %all-reduce.2.cloned.1.call-start = ((), (), s32[]{:S(2)}) async-start(), calls=%async_computation.4 | async-start | bytes 8388608 | tf_op jit(solution)/shard_map/psum | solution.py:122
  710.9 1.6 copy-start.3
  749.0 3.6 copy-start.4
  771.8 41.2 %copy-start.8 = (f32[1024]{0:T(1024)}, f32[1024]{0:T(1024)S(1)}, u32[]{:S(2)}) copy-start(f32[1024]{0:T(1024)S(1)} %psum.15) | copy-start | bytes 12292
  771.8 41.2 %copy-start.1 = (bf16[1024,1024]{1,0:T(8,128)(2,1)S(1)}, bf16[1024,1024]{1,0:T(8,128)(2,1)}, u32[]{:S(2)}) copy-start(bf16[1024,1024]{1,0:T(8,128)(2,1)} %param.10) | copy-start | bytes 6291460
Sparse Core Ops, SparseCore 0:
  10.3 119.2 all-gather.1
  711.1 97.1 all-reduce.1
where the time goes:
time: 832 us; the launch traced here: 820 us
  local copies, waits for them, and re-layouts  398 us (48%)
  waiting for transfers between devices  110 us (13%)
  starting transfers between devices  104 us (12%)
  matrix products  98.9 us (12%)
  blocking collectives  66.1 us (8%)
  other arithmetic  28.1 us (3%)
  between operations  15.1 us (2%)
    gather x1, local copies, waits for them, and re-layouts, body(): jnp.take(all_rows, safe_item // parent_count, axis=0)  240 us
    all_to_all x1, starting transfers between devices, body(): lax.all_to_all(scores, 'clus', split_axis=0, concat_axis=0, tiled=True)  89.5 us
    all_to_all x1, waiting for transfers between devices, body(): lax.all_to_all(scores, 'clus', split_axis=0, concat_axis=0, tiled=True)  46.3 us
    gather x2, local copies, waits for them, and re-layouts, body(): slot_child = jnp.where(filled, all_children.reshape(-1)[safe_item], -1)  45.6 us
    dot_general x2, matrix products, body(): jnp.einsum('sbmd,bcd->sbmc', slot_rows, third[:, child], preferred_elemen...  39.6 us
    psum x1, waiting for transfers between devices, body(): weighted, cluster_mass = lax.psum((partial_sums, partial_mass), 'dp')  36.5 us
    all_gather x1, blocking collectives, body(): lax.all_gather(parents, 'clus', axis=0, tiled=True)  28.2 us
    gather x1, local copies, waits for them, and re-layouts, body(): send_codes = jnp.where(own_filled[:, None], code_items[own_safe], 0.0)  28 us
  transfers between devices with their start and end apart: 5, of which 4 were waited for; matrix products, arithmetic and copies ran while one was open for 24% of the time, Pallas kernels for 0%

commit v1 on v0

--- a/solution.py
+++ b/solution.py
@@ -58,7 +58,9 @@
     own_safe = jnp.maximum(own_item, 0)
     all_rows, all_parents, all_children = (
         lax.all_gather(embeddings, "clus", axis=0, tiled=True),
-        lax.all_gather(parents, "clus", axis=0, tiled=True),
+        jnp.concatenate(
+            lax.all_to_all(jnp.stack([parents] * lax.axis_size("clus")), "clus", 0, 0), axis=0
+        ),
         lax.all_gather(children, "clus", axis=0, tiled=True),
     )
     source_blocks = all_parents.reshape(shard_count, item_count)

time: 832 us -> 813 us (0.977)
  blocking collectives: 66.1 us -> 41.5 us
  starting transfers between devices: 104 us -> 113 us
    all_gather x1 -> x0, blocking collectives: 28.2 us -> none  [body(): lax.all_gather(parents, 'clus', axis=0, tiled=True)]
    sub x3, local copies, waits for them, and re-layouts: 19.2 us -> 6.98 us  [local_ranks(): block_ids - first_block]
    all_to_all x0 -> x1, starting transfers between devices: none -> 9.65 us  [body(): lax.all_to_all(jnp.stack([parents] * lax.axis_size('clus')), 'clus', 0, 0)]
  transfers between devices with their start and end apart: 5 -> 6, of which waited for: 4 -> 4; matrix products, arithmetic and copies ran while one was open for 24% -> 25% of each run, Pallas kernels for 0% -> 0%
where the time goes in v1:
time: 813 us; the launch traced here: 801 us
  local copies, waits for them, and re-layouts  391 us (48%)
  starting transfers between devices  113 us (14%)
  waiting for transfers between devices  110 us (14%)
  matrix products  101 us (12%)
  blocking collectives  41.5 us (5%)
  other arithmetic  30 us (4%)
  between operations  14.8 us (2%)
    gather x1, local copies, waits for them, and re-layouts, body(): jnp.take(all_rows, safe_item // parent_count, axis=0)  240 us
    all_to_all x1, starting transfers between devices, body(): lax.all_to_all(scores, 'clus', split_axis=0, concat_axis=0, tiled=True)  88.7 us
    all_to_all x1, waiting for transfers between devices, body(): lax.all_to_all(scores, 'clus', split_axis=0, concat_axis=0, tiled=True)  46.5 us
    gather x2, local copies, waits for them, and re-layouts, body(): slot_child = jnp.where(filled, all_children.reshape(-1)[safe_item], -1)  45.6 us
    dot_general x2, matrix products, body(): jnp.einsum('sbmd,bcd->sbmc', slot_rows, third[:, child], preferred_elemen...  39.6 us
    psum x1, waiting for transfers between devices, body(): weighted, cluster_mass = lax.psum((partial_sums, partial_mass), 'dp')  36.4 us
    all_gather x1, blocking collectives, body(): lax.all_gather(children, 'clus', axis=0, tiled=True)  29.1 us
    gather x1, local copies, waits for them, and re-layouts, body(): send_codes = jnp.where(own_filled[:, None], code_items[own_safe], 0.0)  28 us
  transfers between devices with their start and end apart: 6, of which 4 were waited for; matrix products, arithmetic and copies ran while one was open for 25% of the time, Pallas kernels for 0%

profile of v1, /device:TPU:1, one launch (start us, length us, event | category | flops | bytes accessed | tf_op | source)
XLA Modules:
  0.0 800.8 jit_solution(14424262593980489277)
XLA Ops:
  9.5 9.6 %all-to-all-start = ((s32[32,512,8]{1,2,0:T(8,128)}), s32[32,512,8]{1,2,0:T(8,128)}, u32[]{:S(2)}, u32[]{:S(2)}) async-start(s32[32,512,8]{1,2,0:T(8,128)} %stack.2), calls=%async_computation | async-start | bytes 1048576 | tf_op jit(solution)/shard_map/all_to_all | solution.py:62
  19.3 29.1 %all_gather.7 = s32[16384,8]{0,1:T(8,128)S(1)} all-gather(s32[512,8]{0,1:T(8,128)} %param.8), channel_id=1, replica_groups=mesh['dp'=4,'clus'=32] {'clus'}, dimensions={0}, use_global_device_ids=true | all-gather | bytes 540672 | tf_op jit(solution)/shard_map/all_gather | solution.py:64
  48.4 5.2 copy.79
  53.6 7.2 reshape.339
  78.2 10.1 %fusion.34 = s32[32,8,32]{2,1,0:T(8,128)S(1)} fusion(f32[4096]{0:T(1024)S(1)} %iota_add_fusion, f32[32,4096]{1,0:T(8,128)} %bitcast.92, s32[32,4096]{1,0:T(8,128)S(1)} %copy.68), kind=kOutput, calls=%fused_computation.55 | convolution fusion | flops 412114944 | bytes 1097728 | tf_op jit(solution)/shard_map/...nb,...nk->...bk/dot_general | solution.py:31
  88.6 45.5 %gather_fusion.2 = s32[8192]{0:T(1024)S(1)} fusion(s32[131072]{0:T(1024)S(1)} %reshape.339, s32[8192]{0:T(1024)S(1)} %broadcast_clamp_fusion.1), kind=kCustom, calls=%fused_computation.2 | custom fusion | bytes 98304 | tf_op jit(solution)/shard_map/gather | solution.py:74
  134.8 240.2 %gather_fusion = bf16[8192,1024]{1,0:T(8,128)(2,1)} fusion(bf16[16384,1024]{1,0:T(8,128)(2,1)} %all-gather.2.cloned.1.call-done, s32[8192]{0:T(1024)S(1)} %broadcast_clamp_fusion.2), kind=kCustom, calls=%fused_computation | custom fusion | bytes 33587200 | tf_op jit(solution)/shard_map/jit(_take)/gather | solution.py:73
  375.0 22.0 %multiply_bitcast_fusion = f32[32,8,32,128]{3,0,2,1:T(8,128)S(1)} fusion(f32[8]{0:T(128)S(1)} %copy-done.8, bf16[8,128,1024,1]{2,1,3,0:T(8,128)(2,1)S(1)} %bitcast.81, bf16[32,8,32,1024]{3,2,1,0:T(8,128)(2,1)} %bitcast.84, pred[32,8,32]{0,2,1:T(8,128)(4,1)S(1)} %copy.74, pred[32,8,32]{0,2,1:T(8,128)(4,1)S(1)} %copy.73), kind=kOutput, calls=%fused_computation.31 | convolution fusion | flops 2165309440 | bytes 23085088 | tf_op jit(solution)/shard_map/sbmd,bcd->sbmc/dot_general | solution.py:78
  401.5 88.7 %all-to-all-start.1 = ((f32[32,8,32,128]{3,2,1,0:T(8,128)}), f32[32,8,32,128]{3,2,1,0:T(8,128)}, u32[]{:S(2)}, u32[]{:S(2)}) async-start(f32[32,8,32,128]{3,2,1,0:T(8,128)} %copy.76), calls=%async_computation.1 | async-start | bytes 8388608 | tf_op jit(solution)/shard_map/all_to_all | solution.py:88
  495.8 46.5 %all-to-all-done.1 = f32[32,8,32,128]{3,2,1,0:T(8,128)} async-done(((f32[32,8,32,128]{3,2,1,0:T(8,128)}), f32[32,8,32,128]{3,2,1,0:T(8,128)}, u32[]{:S(2)}, u32[]{:S(2)}) %all-to-all-start.1) | async-done | bytes 4194336 | tf_op jit(solution)/shard_map/all_to_all | solution.py:88
  542.3 13.0 %gather_fusion.1 = f32[4096,128]{1,0:T(8,128)S(1)} fusion(f32[8192,128]{1,0:T(8,128)} %bitcast.13, s32[4096]{0:T(1024)S(1)} %broadcast_clamp_fusion.3), kind=kCustom, calls=%fused_computation.1 | custom fusion | bytes 4210688 | tf_op jit(solution)/shard_map/gather | solution.py:91
  561.5 28.0 %gather_fusion.4 = f32[8192,128]{1,0:T(8,128)} fusion(f32[4096,128]{1,0:T(8,128)S(1)} %get-tuple-element.7, s32[8192]{0:T(1024)S(1)} %broadcast_clamp_fusion), kind=kCustom, calls=%fused_computation.4 | custom fusion | bytes 8421376 | tf_op jit(solution)/shard_map/gather | solution.py:107
  589.4 5.2 broadcast_select_fusion
  594.7 7.4 all-to-all-start.3
  602.1 21.8 %fusion.21 = f32[8,32,32,128]{3,1,2,0:T(8,128)S(1)} fusion(bf16[8,2,128,1024]{3,2,1,0:T(8,128)(2,1)} %bitcast.101, bf16[32,8,32,1024]{3,2,1,0:T(8,128)(2,1)} %bitcast.85, pred[32,8,32]{0,2,1:T(8,128)(4,1)S(1)} %copy.74, pred[32,8,32]{0,2,1:T(8,128)(4,1)S(1)} %copy.73), kind=kOutput, calls=%fused_computation.41 | convolution fusion | flops 2164260864 | bytes 23085056 | tf_op jit(solution)/shard_map/sbmd,bcd->sbmc/dot_general | solution.py:83
  623.9 17.8 %fusion.12 = f32[32,8,32,128]{3,0,2,1:T(8,128)S(1)} fusion(f32[8,32,32,128]{3,1,2,0:T(8,128)S(1)} %fusion.21, bf16[8,2,128,1024]{3,2,1,0:T(8,128)(2,1)S(1)} %bitcast.102, pred[32,8,32]{0,2,1:T(8,128)(4,1)S(1)} %copy.82, pred[32,8,32]{0,2,1:T(8,128)(4,1)S(1)} %copy.80, bf16[32,8,32,1024]{3,2,1,0:T(8,128)(2,1)} %bitcast.86, pred[32,8,32]{0,2,1:T(8,128)(4,1)S(1)} %copy.74, ...), kind=kOutput, calls=%fused_computation.25 | convolution fusion | flops 2166358016 | bytes 27394048 | tf_op jit(solution)/shard_map/sbmd,bcd->sbmc/dot_general | solution.py:83
  646.2 7.8 all-to-all-done.3
  654.0 7.1 all-to-all-start.2
  666.5 22.2 %fusion.18 = f32[8,256,1024]{2,1,0:T(8,128)S(1)} fusion(bf16[32,8,32,128]{3,0,2,1:T(8,128)(2,1)S(1)} %get-tuple-element.4, bf16[32,8,32,128]{3,0,2,1:T(8,128)(2,1)S(1)} %get-tuple-element.5, bf16[32,8,32,1024]{3,2,1,0:T(8,128)(2,1)} %bitcast.87, pred[32,8,32]{0,2,1:T(8,128)(4,1)S(1)} %copy.74, pred[32,8,32]{0,2,1:T(8,128)(4,1)S(1)} %copy.73), kind=kOutput, calls=%fused_computation.37 | convolution fusion | flops 4320133120 | bytes 29376512 | tf_op jit(solution)/shard_map/sbmc,sbmd->bcd/dot_general | solution.py:119
  694.7 18.5 %all-to-all-done.2 = f32[32,8,32,128]{3,2,1,0:T(8,128)} async-done(((f32[32,8,32,128]{3,2,1,0:T(8,128)}), f32[32,8,32,128]{3,2,1,0:T(8,128)}, u32[]{:S(2)}, u32[]{:S(2)}) %all-to-all-start.2) | async-done | bytes 4194336 | tf_op jit(solution)/shard_map/all_to_all | solution.py:89
  713.2 16.5 %gather_fusion.3 = f32[4096,128]{1,0:T(8,128)} fusion(f32[8192,128]{1,0:T(8,128)} %bitcast.28, s32[4096]{0:T(1024)S(1)} %broadcast_clamp_fusion.3), kind=kCustom, calls=%fused_computation.3 | custom fusion | bytes 4210688 | tf_op jit(solution)/shard_map/gather | solution.py:94
  740.2 12.3 %psum.15 = f32[1024]{0:T(1024)S(1)} all-reduce(f32[1024]{0:T(1024)S(1)} %bitcast.99), channel_id=1, replica_groups=mesh['dp'=4,'clus'=32] {'dp'}, use_global_device_ids=true, to_apply=%region_12.13 | all-reduce | flops 1024 | bytes 8192 | tf_op jit(solution)/shard_map/psum | solution.py:124
  752.6 36.4 %all-reduce.2.cloned.1.call-done = f32[1024,1024]{1,0:T(8,128)} async-done(((f32[1024,1024]{1,0:T(8,128)}), f32[1024,1024]{1,0:T(8,128)}) %all-reduce.2.cloned.1.call-update) | async-done | bytes 4194320 | tf_op jit(solution)/shard_map/psum | solution.py:124
  789.0 4.7 broadcast_divide_fusion
  (94 shorter events, 63.1 us)
Async XLA Ops:
  7.2 367.8 %copy-start = (bf16[1024,1024]{1,0:T(8,128)(2,1)S(1)}, bf16[1024,1024]{1,0:T(8,128)(2,1)}, u32[]{:S(2)}) copy-start(bf16[1024,1024]{1,0:T(8,128)(2,1)} %param.10) | copy-start | bytes 6291460
  7.2 127.6 %all-gather.2.cloned.1.call-start = ((), (), s32[]{:S(2)}) async-start(), calls=%async_computation.4 | async-start | bytes 34603008 | tf_op jit(solution)/shard_map/all_gather | solution.py:60
  9.5 51.3 %all-to-all-start = ((s32[32,512,8]{1,2,0:T(8,128)}), s32[32,512,8]{1,2,0:T(8,128)}, u32[]{:S(2)}, u32[]{:S(2)}) async-start(s32[32,512,8]{1,2,0:T(8,128)} %stack.2), calls=%async_computation | async-start | bytes 1048576 | tf_op jit(solution)/shard_map/all_to_all | solution.py:62
  134.8 240.2 %copy-start.8 = (f32[8]{0:T(128)S(1)}, f32[8]{0:T(128)}, u32[]{:S(2)}) copy-start(f32[8]{0:T(128)} %param.9) | copy-start | bytes 100
  401.5 88.7 %copy-start.5 = (s32[512,8]{0,1:T(8,128)S(1)}, s32[512,8]{0,1:T(8,128)}, u32[]{:S(2)}) copy-start(s32[512,8]{0,1:T(8,128)} %param.7) | copy-start | bytes 49156
  401.5 140.8 %all-to-all-start.1 = ((f32[32,8,32,128]{3,2,1,0:T(8,128)}), f32[32,8,32,128]{3,2,1,0:T(8,128)}, u32[]{:S(2)}, u32[]{:S(2)}) async-start(f32[32,8,32,128]{3,2,1,0:T(8,128)} %copy.76), calls=%async_computation.1 | async-start | bytes 8388608 | tf_op jit(solution)/shard_map/all_to_all | solution.py:88
  555.3 3.0 copy-start.2
  594.7 59.4 %all-to-all-start.3 = ((f32[32,256,128]{2,1,0:T(8,128)}), f32[32,256,128]{2,1,0:T(8,128)}, u32[]{:S(2)}, u32[]{:S(2)}) async-start(f32[32,256,128]{2,1,0:T(8,128)} %broadcast_select_fusion), calls=%async_computation.3 | async-start | bytes 8388608 | tf_op jit(solution)/shard_map/all_to_all | solution.py:108
  602.1 21.8 %copy-start.7 = (bf16[2048,1024]{1,0:T(8,128)(2,1)S(1)}, bf16[2048,1024]{1,0:T(8,128)(2,1)}, u32[]{:S(2)}) copy-start(bf16[2048,1024]{1,0:T(8,128)(2,1)} %param.11) | copy-start | bytes 12582916
  654.0 59.2 %all-to-all-start.2 = ((f32[32,8,32,128]{3,2,1,0:T(8,128)}), f32[32,8,32,128]{3,2,1,0:T(8,128)}, u32[]{:S(2)}, u32[]{:S(2)}) async-start(f32[32,8,32,128]{3,2,1,0:T(8,128)} %copy.84), calls=%async_computation.2 | async-start | bytes 8388608 | tf_op jit(solution)/shard_map/all_to_all | solution.py:89
  661.1 127.9 %all-reduce.2.cloned.1.call-start = ((), (), s32[]{:S(2)}) async-start(), calls=%async_computation.5 | async-start | bytes 8388608 | tf_op jit(solution)/shard_map/psum | solution.py:124
  691.6 1.6 copy-start.3
  729.7 3.6 copy-start.4
  752.6 41.1 %copy-start.6 = (f32[1024]{0:T(1024)}, f32[1024]{0:T(1024)S(1)}, u32[]{:S(2)}) copy-start(f32[1024]{0:T(1024)S(1)} %psum.15) | copy-start | bytes 12292
  752.6 41.1 %copy-start.1 = (bf16[1024,1024]{1,0:T(8,128)(2,1)S(1)}, bf16[1024,1024]{1,0:T(8,128)(2,1)}, u32[]{:S(2)}) copy-start(bf16[1024,1024]{1,0:T(8,128)(2,1)} %param.10) | copy-start | bytes 6291460
Sparse Core Ops, SparseCore 0:
  10.3 118.7 all-gather.1
  691.8 97.2 all-reduce.1
